TPU v7x, 32 devices: a whole 2x2x4 slice. The times are simulated.
32 devices in a mesh: dp: 16 (over z, x, core), head: 2 (over y).
Axes of the slice: x: 2, y: 2, z: 4, core: 2. Of those that a mesh axis runs over, the one named last changes fastest.
Arguments:
- tokens: bfloat16 [32768, 512], P(('dp', 'head')), may hold values from -6 to 6
- lengths: int32 [128], P('dp'), may hold values from 40 to 256, as said below
- ln1_gain: float32 [512], replicated, may hold values from 0.5 to 1.5
- ln1_bias: float32 [512], replicated, may hold values from -1 to 1
- w_query: bfloat16 [512, 512], P(None, 'head'), may hold values from -0.25 to 0.25
- w_key: bfloat16 [512, 512], P(None, 'head'), may hold values from -0.25 to 0.25
- w_value: bfloat16 [512, 512], P(None, 'head'), may hold values from -0.25 to 0.25
- w_out: bfloat16 [512, 512], P('head'), may hold values from -1 to 1
- sort_first: bfloat16 [512, 512], replicated, may hold values from -0.25 to 0.25
- sort_second: bfloat16 [512, 8], replicated, may hold values from -0.5 to 0.5
- ln2_gain: float32 [512], replicated, may hold values from 0.5 to 1.5
- ln2_bias: float32 [512], replicated, may hold values from -1 to 1
- w_up: bfloat16 [512, 2048], replicated, may hold values from -0.25 to 0.25
- w_down: bfloat16 [2048, 512], replicated, may hold values from -0.125 to 0.125
- cotangent: bfloat16 [32768, 512], P(('dp', 'head')), may hold values from -6 to 6
Outputs:
- output: bfloat16 [32768, 512], P(('dp', 'head'))
- input_grad: bfloat16 [32768, 512], P(('dp', 'head'))
- grad_ln1_gain: float32 [512], replicated
- grad_ln1_bias: float32 [512], replicated
- grad_query: float32 [512, 512], P(None, 'head')
- grad_key: float32 [512, 512], P(None, 'head')
- grad_value: float32 [512, 512], P(None, 'head')
- grad_out: float32 [512, 512], P('head')
- grad_sort_first: float32 [512, 512], replicated
- grad_sort_second: float32 [512, 8], replicated
- grad_ln2_gain: float32 [512], replicated
- grad_ln2_bias: float32 [512], replicated
- grad_up: float32 [512, 2048], replicated
- grad_down: float32 [2048, 512], replicated
Inputs may be any that keep to these rules, and one draw needn't show every extreme that they name: `lengths`: some sequence has exactly 256 valid tokens and some has exactly 40.
All inputs are finite; a program needn't handle non-finite values.
Results may differ from a plain program's by a relative error of at most 0.017.
Values may be sent and summed in bfloat16 or wider, within the bound.
No kernel may reach another device: no remote copies, remote signals or barrier semaphores. Data moves between devices by JAX's collectives and lax.ppermute only.
A program may use at most 192 MiB of HBM per device.

v0:
```python
import jax
import jax.numpy as jnp
from jax import lax
from jax.sharding import PartitionSpec as P

HD = 64
BL = 32
ITERS = 8
LMAX = 256
precise = lax.Precision.HIGHEST


def smooth_gate(values):
    return jax.nn.gelu(values, approximate=False)


def layer_norm(values, gain_vec, bias_vec):
    center = values - jnp.mean(values, axis=-1, keepdims=True)
    spread = jnp.mean(center * center, axis=-1, keepdims=True)
    return center * lax.rsqrt(spread + 1e-05) * gain_vec + bias_vec


def log_total(values, along):
    row_top = jnp.max(values, axis=along, keepdims=True)
    return row_top + jnp.log(jnp.sum(jnp.exp(values - row_top), axis=along, keepdims=True))


def sort_plan(summary, sort_one, sort_two, block_ok):
    hidden = smooth_gate(jnp.einsum("cid,de->cie", summary, sort_one, precision=precise))
    logits = jnp.einsum("cie,ej->cij", hidden, sort_two, precision=precise)
    diagonal = jnp.eye(logits.shape[1], dtype=jnp.bool_)[None]
    allowed = block_ok[:, :, None] & block_ok[:, None, :] | diagonal & ~block_ok[:, :, None]
    plan_log = jnp.where(allowed, logits, -1e30)
    for sweep_index in range(ITERS):
        plan_log = plan_log - log_total(plan_log, 2)
        plan_log = plan_log - log_total(plan_log, 1)
    return jnp.exp(plan_log)


def outer_product(left, right):
    return lax.dot_general(
        left, right, (((0,), (0,)), ((), ())), preferred_element_type=jnp.float32
    )


def attend_forward(queries, key_rows, value_rows, soft_plan, tok_ok, block_ok):
    tok_mask = tok_ok[..., None, None].astype(jnp.bfloat16)
    key_kept = key_rows * tok_mask
    value_kept = value_rows * tok_mask
    sorted_keys = jnp.einsum(
        "cij,cjthd->cithd", soft_plan, key_kept.astype(jnp.float32), precision=precise
    ).astype(jnp.bfloat16)
    sorted_values = jnp.einsum(
        "cij,cjthd->cithd", soft_plan, value_kept.astype(jnp.float32), precision=precise
    ).astype(jnp.bfloat16)
    all_keys = jnp.concatenate([key_kept, sorted_keys], axis=2)
    all_values = jnp.concatenate([value_kept, sorted_values], axis=2)
    score_scale = queries.shape[-1] ** (-0.5)
    scores = (
        jnp.einsum("cibhd,cikhd->cihbk", queries, all_keys, preferred_element_type=jnp.float32)
        * score_scale
    )
    key_ok = jnp.concatenate([tok_ok, jnp.broadcast_to(block_ok[:, :, None], tok_ok.shape)], axis=2)
    allowed = key_ok[:, :, None, None, :] | ~tok_ok[:, :, None, :, None]
    scores = jnp.where(allowed, scores, -1e30)
    weights = jnp.exp(scores - log_total(scores, 4))
    weights_low = weights.astype(jnp.bfloat16)
    mixed_rows = jnp.einsum(
        "cihbk,cikhd->cibhd", weights_low, all_values, preferred_element_type=jnp.float32
    )
    mixed_rows = mixed_rows * tok_ok[..., None, None].astype(jnp.float32)
    return (mixed_rows, (key_kept, all_keys, all_values, weights, weights_low))


def attend_backward(grad_mixed, queries, soft_plan, tok_ok, saved_state):
    key_kept, all_keys, all_values, weights, weights_low = saved_state
    block_len = key_kept.shape[2]
    score_scale = queries.shape[-1] ** (-0.5)
    value_kept = all_values[:, :, :block_len]
    grad_rows = grad_mixed * tok_ok[..., None, None].astype(jnp.bfloat16)
    grad_weights = jnp.einsum(
        "cibhd,cikhd->cihbk", grad_rows, all_values, preferred_element_type=jnp.float32
    )
    grad_all_values = jnp.einsum(
        "cihbk,cibhd->cikhd", weights_low, grad_rows, preferred_element_type=jnp.float32
    )
    weighted = jnp.sum(weights * grad_weights, axis=4, keepdims=True)
    grad_scores = (weights * (grad_weights - weighted)).astype(jnp.bfloat16)
    grad_queries = (
        jnp.einsum("cihbk,cikhd->cibhd", grad_scores, all_keys, preferred_element_type=jnp.float32)
        * score_scale
    )
    grad_all_keys = (
        jnp.einsum("cihbk,cibhd->cikhd", grad_scores, queries, preferred_element_type=jnp.float32)
        * score_scale
    )
    grad_sorted_keys = grad_all_keys[:, :, block_len:]
    grad_sorted_values = grad_all_values[:, :, block_len:]
    grad_plan = jnp.einsum(
        "cithd,cjthd->cij", grad_sorted_keys, key_kept.astype(jnp.float32), precision=precise
    )
    grad_plan = grad_plan + jnp.einsum(
        "cithd,cjthd->cij", grad_sorted_values, value_kept.astype(jnp.float32), precision=precise
    )
    key_total = grad_all_keys[:, :, :block_len] + jnp.einsum(
        "cij,cithd->cjthd", soft_plan, grad_sorted_keys, precision=precise
    )
    value_total = grad_all_values[:, :, :block_len] + jnp.einsum(
        "cij,cithd->cjthd", soft_plan, grad_sorted_values, precision=precise
    )
    tok_mask = tok_ok[..., None, None].astype(jnp.float32)
    return (
        grad_queries.astype(jnp.bfloat16),
        (key_total * tok_mask).astype(jnp.bfloat16),
        (value_total * tok_mask).astype(jnp.bfloat16),
        grad_plan,
    )


def run_attention(normed_here, span_list, query_cols, key_cols, value_cols, sort_one, sort_two):
    seq_count = span_list.shape[0]
    nblocks = LMAX // BL
    heads_here = query_cols.shape[1] // HD
    positions = jnp.arange(LMAX, dtype=jnp.int32)
    tok_ok = (positions[None, :] < span_list[:, None]).reshape(seq_count, nblocks, BL)
    block_ok = (jnp.arange(nblocks, dtype=jnp.int32) * BL)[None, :] < span_list[:, None]
    block_shape = (seq_count, nblocks, BL, heads_here, HD)
    queries = (
        jnp.dot(normed_here, query_cols, preferred_element_type=jnp.float32)
        .astype(jnp.bfloat16)
        .reshape(block_shape)
    )
    key_rows = (
        jnp.dot(normed_here, key_cols, preferred_element_type=jnp.float32)
        .astype(jnp.bfloat16)
        .reshape(block_shape)
    )
    value_rows = (
        jnp.dot(normed_here, value_cols, preferred_element_type=jnp.float32)
        .astype(jnp.bfloat16)
        .reshape(block_shape)
    )
    summary = jnp.sum(
        normed_here.reshape(seq_count, nblocks, BL, -1).astype(jnp.float32) * tok_ok[..., None],
        axis=2,
    ) * BL ** (-0.5)

    def plan_of(summary_in, first_in, second_in):
        return sort_plan(summary_in, first_in, second_in, block_ok)

    soft_plan, plan_back = jax.vjp(plan_of, summary, sort_one, sort_two)
    mixed_rows, saved_state = attend_forward(
        queries, key_rows, value_rows, soft_plan, tok_ok, block_ok
    )
    mixed_rows = mixed_rows.reshape(normed_here.shape[0], -1).astype(jnp.bfloat16)
    return (mixed_rows, queries, tok_ok, soft_plan, plan_back, saved_state)


def on_device(
    tokens,
    lengths,
    ln1_gain,
    ln1_bias,
    w_query,
    w_key,
    w_value,
    w_out,
    sort_first,
    sort_second,
    ln2_gain,
    ln2_bias,
    w_up,
    w_down,
    cotangent,
):
    head_side = lax.axis_index("head")
    local_rows = tokens.shape[0]
    inputs = tokens.astype(jnp.float32)
    sort_one = sort_first.astype(jnp.float32)
    sort_two = sort_second.astype(jnp.float32)
    normed_f, norm_back = jax.vjp(layer_norm, inputs, ln1_gain, ln1_bias)
    normed = normed_f.astype(jnp.bfloat16)
    normed_here = lax.all_gather(normed, "head", axis=0, tiled=True)
    query_cols, key_cols, value_cols, out_rows = (w_query, w_key, w_value, w_out)
    sort_share = (head_side == 0).astype(jnp.float32)
    mixed_rows, queries, tok_ok, soft_plan, plan_back, saved_state = run_attention(
        normed_here, lengths, query_cols, key_cols, value_cols, sort_one, sort_two
    )
    attention = lax.psum_scatter(
        jnp.dot(mixed_rows, w_out, preferred_element_type=jnp.float32).astype(jnp.bfloat16),
        "head",
        scatter_dimension=0,
        tiled=True,
    ).astype(jnp.float32)
    middle = inputs + attention
    normed_two_f, norm_two_back = jax.vjp(layer_norm, middle, ln2_gain, ln2_bias)
    normed_two = normed_two_f.astype(jnp.bfloat16)
    up_value = jnp.dot(normed_two, w_up, preferred_element_type=jnp.float32)
    hidden_f, gate_back = jax.vjp(smooth_gate, up_value)
    hidden = hidden_f.astype(jnp.bfloat16)
    output = (middle + jnp.dot(hidden, w_down, preferred_element_type=jnp.float32)).astype(
        jnp.bfloat16
    )
    grad_hidden = jnp.dot(cotangent, w_down.T, preferred_element_type=jnp.float32).astype(
        jnp.bfloat16
    )
    grad_upin = gate_back(grad_hidden.astype(jnp.float32))[0].astype(jnp.bfloat16)
    grad_down = outer_product(hidden, cotangent)
    grad_up = outer_product(normed_two, grad_upin)
    grad_middle_norm, grad_gain_two, grad_bias_two = norm_two_back(
        jnp.dot(grad_upin, w_up.T, preferred_element_type=jnp.float32)
    )
    grad_middle = cotangent.astype(jnp.float32) + grad_middle_norm
    grad_attention = grad_middle.astype(jnp.bfloat16)
    grad_attention_here = lax.all_gather(grad_attention, "head", axis=0, tiled=True)
    grad_w_out = outer_product(mixed_rows, grad_attention_here)
    grad_mixed = jnp.dot(
        grad_attention_here, out_rows.T, preferred_element_type=jnp.float32
    ).astype(jnp.bfloat16)
    grad_queries, grad_keys, grad_values, grad_plan = attend_backward(
        grad_mixed.reshape(queries.shape), queries, soft_plan, tok_ok, saved_state
    )
    grad_plan = lax.psum(grad_plan, "head")
    grad_summary, grad_first, grad_second = plan_back(grad_plan)
    rows_here = normed_here.shape[0]
    grad_queries = grad_queries.reshape(rows_here, -1)
    grad_keys = grad_keys.reshape(rows_here, -1)
    grad_values = grad_values.reshape(rows_here, -1)
    grad_spread = (grad_summary[:, :, None, :] * tok_ok[..., None] * BL ** (-0.5)).reshape(
        rows_here, -1
    )
    grad_w_query = outer_product(normed_here, grad_queries)
    grad_w_key = outer_product(normed_here, grad_keys)
    grad_w_value = outer_product(normed_here, grad_values)
    total_term = jnp.dot(grad_queries, w_query.T, preferred_element_type=jnp.float32)
    total_term = total_term + jnp.dot(grad_keys, w_key.T, preferred_element_type=jnp.float32)
    grad_normed = lax.psum_scatter(
        (total_term + jnp.dot(grad_values, w_value.T, preferred_element_type=jnp.float32)).astype(
            jnp.bfloat16
        ),
        "head",
        scatter_dimension=0,
        tiled=True,
    ).astype(jnp.float32)
    grad_normed = grad_normed + lax.dynamic_slice_in_dim(
        grad_spread, head_side * local_rows, local_rows, 0
    )
    grad_w_query, grad_w_key, grad_w_value, grad_w_out = lax.psum(
        (grad_w_query, grad_w_key, grad_w_value, grad_w_out), "dp"
    )
    grad_inputs_norm, grad_gain_one, grad_bias_one = norm_back(grad_normed)
    input_grad = (grad_middle + grad_inputs_norm).astype(jnp.bfloat16)
    summed = lax.psum(
        (
            grad_gain_one,
            grad_bias_one,
            grad_first * sort_share,
            grad_second * sort_share,
            grad_gain_two,
            grad_bias_two,
            grad_up,
            grad_down,
        ),
        ("dp", "head"),
    )
    return (
        output,
        input_grad,
        summed[0],
        summed[1],
        grad_w_query,
        grad_w_key,
        grad_w_value,
        grad_w_out,
        summed[2],
        summed[3],
        summed[4],
        summed[5],
        summed[6],
        summed[7],
    )


def solution(mesh):
    return jax.shard_map(
        on_device,
        mesh=mesh,
        in_specs=(
            P(("dp", "head"), None),
            P("dp"),
            P(),
            P(),
            P(None, "head"),
            P(None, "head"),
            P(None, "head"),
            P("head", None),
            P(),
            P(),
            P(),
            P(),
            P(),
            P(),
            P(("dp", "head"), None),
        ),
        out_specs=(
            P(("dp", "head"), None),
            P(("dp", "head"), None),
            P(),
            P(),
            P(None, "head"),
            P(None, "head"),
            P(None, "head"),
            P("head", None),
            P(),
            P(),
            P(),
            P(),
            P(),
            P(),
        ),
        check_vma=False,
    )
```

profile of v0, /device:TPU:0, one launch (start us, length us, event | category | flops | bytes accessed | tf_op | source)
XLA Modules:
  0.0 688.6 jit_solution(9410272883061867089)
XLA Ops:
  16.0 33.3 %all-gather.3.cloned.1.call-done = bf16[2048,512]{1,0:T(8,128)(2,1)} async-done(((bf16[1024,512]{1,0:T(8,128)(2,1)}), bf16[2048,512]{1,0:T(8,128)(2,1)}) %all-gather.3.cloned.1.call-update) | async-done | bytes 2097168 | tf_op jit(solution)/shard_map/all_gather | solution.py:183
  70.4 4.6 reshape.615
  78.3 4.4 reshape.614
  86.8 4.9 copy_multiply_fusion.1
  107.4 4.4 convert_element_type.198
  115.2 31.9 %reduce-scatter.3.cloned.1.call-done = bf16[1024,512]{1,0:T(8,128)(2,1)} async-done(((bf16[2048,512]{1,0:T(8,128)(2,1)}), bf16[1024,512]{1,0:T(8,128)(2,1)}) %reduce-scatter.3.cloned.1.call-update) | async-done | bytes 1048592 | tf_op jit(solution)/shard_map/reduce_scatter | solution.py:189
  150.6 23.5 %multiply_convert_fusion = (bf16[1024,2048]{1,0:T(8,128)(2,1)}, f32[1024,2048]{1,0:T(8,128)S(1)}, f32[1024,2048]{1,0:T(8,128)}) fusion(bf16[512,2048]{1,0:T(8,128)(2,1)S(1)} %copy-done, bf16[1024,512]{1,0:T(8,128)(2,1)S(1)} %copy-done.26, bf16[1024,512]{1,0:T(8,128)(2,1)S(1)} %copy-done.2, f32[512]{0:T(512)} %param.26, f32[512]{0:T(512)} %param.25, ...), kind=kOutput, calls=%fused_computation.12 | convolution fusion | flops 2287992832 | bytes 25178112 | tf_op jit(solution)/shard_map/dot_general | solution.py:198
  174.0 6.9 %fusion.5 = bf16[1024,2048]{1,0:T(8,128)(2,1)S(1)} fusion(f32[1024,2048]{1,0:T(8,128)S(1)} %get-tuple-element.86, f32[1024,2048]{1,0:T(8,128)} %get-tuple-element.110, bf16[1024,512]{1,0:T(8,128)(2,1)S(1)} %copy-done.36, bf16[2048,512]{1,0:T(8,128)(2,1)S(1)} %copy-done.156), kind=kOutput, calls=%fused_computation.8 | convolution fusion | flops 2181038080 | bytes 24117248 | tf_op jit(solution)/shard_map/dot_general | solution.py:204
  187.3 6.9 %fusion.167 = f32[2048,512]{1,0:T(8,128)} fusion(bf16[1024,2048]{1,0:T(8,128)(2,1)} %get-tuple-element.85, bf16[1024,512]{1,0:T(8,128)(2,1)} %param.29), kind=kOutput, calls=%fused_computation.381 | convolution fusion | flops 2147483648 | bytes 9437184 | tf_op jit(solution)/shard_map/dot_general | solution.py:41
  194.3 4.6 fusion.143
  198.9 21.4 %all-gather.5.cloned.1.call-done = bf16[2048,512]{1,0:T(8,128)(2,1)} async-done(((bf16[1024,512]{1,0:T(8,128)(2,1)}), bf16[2048,512]{1,0:T(8,128)(2,1)}) %all-gather.5.cloned.1.call-update) | async-done | bytes 2097168 | tf_op jit(solution)/shard_map/all_gather | solution.py:215
  227.5 7.2 %multiply_reduce_fusion = (f32[8,8,4,32]{3,2,1,0:T(4,128)S(1)}, f32[8,8,4,32,64]{4,3,2,1,0:T(8,128)S(1)}) fusion(f32[8,8,4,32,64]{4,3,2,1,0:T(8,128)S(1)} %copy-done.4, f32[8,8,4,32]{3,2,1,0:T(4,128)} %bitcast.104, pred[8,8,32,64]{3,2,1,0:T(8,128)(4,1)S(1)} %broadcast_or_fusion, bf16[8,8,64,4,64]{4,1,3,2,0:T(8,128)(2,1)} %copy-done.35, ...), kind=kOutput, calls=%fused_computation.47 | convolution fusion | flops 69722112 | bytes 7536640 | tf_op jit(solution)/shard_map/cibhd,cikhd->cihbk/dot_general | solution.py:81
  234.7 5.8 convolution_bitcast_fusion
  249.8 6.4 fusion.65
  256.2 7.6 %fusion.24 = f32[8,8,32,4,64]{4,1,3,2,0:T(8,128)} fusion(f32[8,8,32,4,64]{4,2,3,1,0:T(8,128)S(1)} %slice.17, f32[8,8,8]{2,1,0:T(8,128)S(1)} %get-tuple-element.88, f32[8,8]{1,0:T(8,128)S(1)} %log_add_fusion.1, f32[8,8]{1,0:T(8,128)S(1)} %log_add_fusion.2), kind=kOutput, calls=%fused_computation.42 | convolution fusion | flops 50332672 | bytes 4196864 | tf_op jit(solution)/shard_map/cij,cithd->cjthd/dot_general | solution.py:105
  275.5 7.2 %fusion.22 = f32[8,8,32,4,64]{4,1,3,2,0:T(8,128)} fusion(f32[8,8,32,4,64]{4,2,3,1,0:T(8,128)S(1)} %slice.19, f32[8,8,8]{2,1,0:T(8,128)S(1)} %get-tuple-element.88, f32[8,8]{1,0:T(8,128)S(1)} %log_add_fusion.1, f32[8,8]{1,0:T(8,128)S(1)} %log_add_fusion.2), kind=kOutput, calls=%fused_computation.40 | convolution fusion | flops 50332672 | bytes 4196864 | tf_op jit(solution)/shard_map/cij,cithd->cjthd/dot_general | solution.py:108
  282.6 5.5 fusion.75
  288.2 7.2 %psum.91 = f32[8,8,8]{2,1,0:T(8,128)S(1)} all-reduce(f32[8,8,8]{2,1,0:T(8,128)S(1)} %fusion.75), channel_id=1, replica_groups=mesh['dp'=16,'head'=2] {'head'}, use_global_device_ids=true, to_apply=%region_44.45 | all-reduce | flops 512 | bytes 4096 | tf_op jit(solution)/shard_map/psum | solution.py:223
  295.4 12.7 %fusion.14 = (bf16[8,8,32,4,64]{4,2,3,1,0:T(8,128)(2,1)S(1)}, bf16[8,8,32,4,64]{4,2,3,1,0:T(8,128)(2,1)}) fusion(f32[8,8,64,4,64]{4,2,3,1,0:T(8,128)} %convolution_bitcast_fusion, f32[8,8,32,4,64]{4,1,3,2,0:T(8,128)} %fusion.22, f32[8,8,32]{2,1,0:T(8,128)S(1)} %get-tuple-element.101, f32[8,8,32,4,64]{4,1,3,2,0:T(8,128)} %fusion.24, ...), kind=kLoop, calls=%fused_computation.28 | loop fusion | flops 3145728 | bytes 10493952 | tf_op jit(solution)/shard_map/convert_element_type | solution.py:115
  346.0 6.3 add_convert_fusion.2
  354.0 10.0 %reduce-scatter.5.cloned.1.call-done = bf16[1024,512]{1,0:T(8,128)(2,1)} async-done(((bf16[2048,512]{1,0:T(8,128)(2,1)}), bf16[1024,512]{1,0:T(8,128)(2,1)}) %reduce-scatter.5.cloned.1.call-update) | async-done | bytes 1048592 | tf_op jit(solution)/shard_map/reduce_scatter | solution.py:237
  367.6 40.3 %all-reduce = (f32[512]{0:T(512)}, f32[512]{0:T(512)}, f32[512,8]{0,1:T(8,128)}, f32[512]{0:T(512)}, f32[512]{0:T(512)}) all-reduce(f32[512]{0:T(512)S(1)} %get-tuple-element.16, f32[512]{0:T(512)S(1)} %get-tuple-element.19, f32[512,8]{0,1:T(8,128)S(1)} %fusion.80, ...), channel_id=1, replica_groups=mesh['dp'=16,'head'=2] {'dp','head'}, use_global_device_ids=true, to_apply=%region_96.97 | all-reduce | flops 6144 | bytes 49152 | tf_op jit(solution)/shard_map/psum | solution.py:253
  411.1 55.9 %all-reduce.8.cloned.1.call-done = (f32[512,256]{1,0:T(8,128)}, f32[512,256]{1,0:T(8,128)}, f32[512,256]{1,0:T(8,128)}, f32[256,512]{1,0:T(8,128)}) async-done(((f32[512,256]{1,0:T(8,128)}, f32[512,256]{1,0:T(8,128)}, f32[512,256]{1,0:T(8,128)}, f32[256,512]{1,0:T(8,128)}), (f32[512,256]{1,0:T(8,128)}, f32[512,256]{1,0:T(8,128)}, f32[512,256]{1,0:T(8,128)}, ...) | async-done | bytes 2097168 | tf_op jit(solution)/shard_map/psum | solution.py:248
  467.0 198.9 %all-reduce.6.cloned.1.call-done = (f32[512,512]{1,0:T(8,128)}, f32[512,2048]{1,0:T(8,128)}, f32[2048,512]{1,0:T(8,128)}) async-done(((f32[512,512]{1,0:T(8,128)}, f32[512,2048]{1,0:T(8,128)}, f32[2048,512]{1,0:T(8,128)}), (f32[512,512]{1,0:T(8,128)}, f32[512,2048]{1,0:T(8,128)}, f32[2048,512]{1,0:T(8,128)})) %all-reduce.6.cloned.1.call-update) | async-done | bytes 9437200 | tf_op jit(solution)/shard_map/psum | solution.py:253
  (524 shorter events, 153.7 us)
Async XLA Ops:
  7.2 143.3 %copy-start = (bf16[512,2048]{1,0:T(8,128)(2,1)S(1)}, bf16[512,2048]{1,0:T(8,128)(2,1)}, u32[]{:S(2)}) copy-start(bf16[512,2048]{1,0:T(8,128)(2,1)} %param.27) | copy-start | bytes 6291460
  7.2 45.0 %copy-start.50 = (bf16[512,512]{1,0:T(8,128)(2,1)S(1)}, bf16[512,512]{1,0:T(8,128)(2,1)}, u32[]{:S(2)}) copy-start(bf16[512,512]{1,0:T(8,128)(2,1)} %param.23) | copy-start | bytes 1572868
  7.2 42.1 %all-gather.3.cloned.1.call-start = ((), (), s32[]{:S(2)}) async-start(), calls=%async_computation.2 | async-start | bytes 3145728 | tf_op jit(solution)/shard_map/all_gather | solution.py:183
  8.9 44.3 %copy-start.149 = (bf16[512,8]{0,1:T(8,128)(2,1)S(1)}, bf16[512,8]{0,1:T(8,128)(2,1)}, u32[]{:S(2)}) copy-start(bf16[512,8]{0,1:T(8,128)(2,1)} %param.24) | copy-start | bytes 24580
  8.9 40.4 %copy-start.68 = (f32[1024]{0:T(1024)}, f32[1024]{0:T(1024)S(1)}, u32[]{:S(2)}) copy-start(f32[1024]{0:T(1024)S(1)} %broadcast_multiply_fusion.1) | copy-start | bytes 12292
  10.6 38.7 %copy-start.111 = (f32[1024]{0:T(1024)}, f32[1024]{0:T(1024)S(1)}, u32[]{:S(2)}) copy-start(f32[1024]{0:T(1024)S(1)} %fusion.45) | copy-start | bytes 12292
  10.6 38.7 %copy-start.107 = (f32[1024]{0:T(1024)}, f32[1024]{0:T(1024)S(1)}, u32[]{:S(2)}) copy-start(f32[1024]{0:T(1024)S(1)} %fusion.127) | copy-start | bytes 12292
  13.3 133.8 %reduce-scatter.3.cloned.1.call-start = ((), (), s32[]{:S(2)}) async-start(), calls=%async_computation.3 | async-start | bytes 3145728 | tf_op jit(solution)/shard_map/reduce_scatter | solution.py:189
  13.5 281.9 %copy-start.48 = (f32[8,8,32]{2,1,0:T(8,128)}, f32[8,8,32]{2,1,0:T(8,128)S(1)}, u32[]{:S(2)}) copy-start(f32[8,8,32]{2,1,0:T(8,128)S(1)} %get-tuple-element.101) | copy-start | bytes 24580
  49.3 18.4 %copy-start.5 = (bf16[2048,512]{1,0:T(8,128)(2,1)S(1)}, bf16[2048,512]{1,0:T(8,128)(2,1)}, u32[]{:S(2)}) copy-start(bf16[2048,512]{1,0:T(8,128)(2,1)} %all-gather.3.cloned.1.call-done) | copy-start | bytes 6291460
  52.6 22.3 %copy-start.52 = (f32[8,8,512]{2,1,0:T(8,128)}, f32[8,8,512]{2,1,0:T(8,128)S(1)}, u32[]{:S(2)}) copy-start(f32[8,8,512]{2,1,0:T(8,128)S(1)} %get-tuple-element.105) | copy-start | bytes 393220
  53.1 21.9 %copy-start.54 = (f32[8,8,512]{2,1,0:T(8,128)}, f32[8,8,512]{2,1,0:T(8,128)S(1)}, u32[]{:S(2)}) copy-start(f32[8,8,512]{2,1,0:T(8,128)S(1)} %fusion.85) | copy-start | bytes 393220
  58.0 16.9 %copy-start.20 = (f32[8,8,8]{2,1,0:T(8,128)}, f32[8,8,8]{2,1,0:T(8,128)S(1)}, u32[]{:S(2)}) copy-start(f32[8,8,8]{2,1,0:T(8,128)S(1)} %get-tuple-element.94) | copy-start | bytes 6148
  61.0 14.0 %copy-start.22 = (f32[8,8,8]{2,1,0:T(8,128)}, f32[8,8,8]{2,1,0:T(8,128)S(1)}, u32[]{:S(2)}) copy-start(f32[8,8,8]{2,1,0:T(8,128)S(1)} %get-tuple-element.92) | copy-start | bytes 6148
  61.6 13.4 %copy-start.46 = (f32[8,8]{1,0:T(8,128)}, f32[8,8]{1,0:T(8,128)S(1)}, u32[]{:S(2)}) copy-start(f32[8,8]{1,0:T(8,128)S(1)} %log_add_fusion.8) | copy-start | bytes 772
  107.4 39.7 %copy-start.2 = (bf16[1024,512]{1,0:T(8,128)(2,1)S(1)}, bf16[1024,512]{1,0:T(8,128)(2,1)}, u32[]{:S(2)}) copy-start(bf16[1024,512]{1,0:T(8,128)(2,1)} %param.15) | copy-start | bytes 3145732
  115.1 105.2 %all-gather.5.cloned.1.call-start = ((), (), s32[]{:S(2)}) async-start(), calls=%async_computation.4 | async-start | bytes 3145728 | tf_op jit(solution)/shard_map/all_gather | solution.py:215
  150.5 33.8 %copy-start.147 = (f32[1024]{0:T(1024)}, f32[1024]{0:T(1024)S(1)}, u32[]{:S(2)}) copy-start(f32[1024]{0:T(1024)S(1)} %fusion.128) | copy-start | bytes 12292
  150.5 23.5 %copy-start.36 = (bf16[1024,512]{1,0:T(8,128)(2,1)S(1)}, bf16[1024,512]{1,0:T(8,128)(2,1)}, u32[]{:S(2)}) copy-start(bf16[1024,512]{1,0:T(8,128)(2,1)} %param.29) | copy-start | bytes 3145732
  150.5 23.5 %copy-start.156 = (bf16[2048,512]{1,0:T(8,128)(2,1)S(1)}, bf16[2048,512]{1,0:T(8,128)(2,1)}, u32[]{:S(2)}) copy-start(bf16[2048,512]{1,0:T(8,128)(2,1)} %param.28) | copy-start | bytes 6291460
  187.0 177.0 %reduce-scatter.5.cloned.1.call-start = ((), (), s32[]{:S(2)}) async-start(), calls=%async_computation.5 | async-start | bytes 3145728 | tf_op jit(solution)/shard_map/reduce_scatter | solution.py:237
  314.3 12.5 %copy-start.24 = (bf16[2048,256]{1,0:T(8,128)(2,1)}, bf16[2048,256]{1,0:T(8,128)(2,1)S(1)}, u32[]{:S(2)}) copy-start(bf16[2048,256]{1,0:T(8,128)(2,1)S(1)} %reshape.619) | copy-start | bytes 3145732
  330.9 136.2 %all-reduce.8.cloned.1.call-start = ((), (), s32[]{:S(2)}) async-start(), calls=%async_computation.7 | async-start | bytes 4194304 | tf_op jit(solution)/shard_map/psum | solution.py:248
  340.5 325.5 %all-reduce.6.cloned.1.call-start = ((), (), s32[]{:S(2)}) async-start(), calls=%async_computation.6 | async-start | bytes 18874368 | tf_op jit(solution)/shard_map/psum | solution.py:253
  (143 other events, 639.9 us)
Sparse Core Ops, SparseCore 0:
  13.4 35.8 all-gather.2
  115.2 31.8 reduce-scatter.2
  187.1 33.1 all-gather.4
  331.0 33.0 reduce-scatter.4
  368.4 98.5 all-reduce.7
  474.6 191.2 all-reduce.5
where the time goes:
time: 695 us; the launch traced here: 689 us
  waiting for transfers between devices  352 us (51%)
  matrix products  137 us (20%)
  local copies, waits for them, and re-layouts  75.9 us (11%)
  other arithmetic  58.7 us (8%)
  blocking collectives  47.5 us (7%)
  between operations  17.1 us (2%)
    psum x1, waiting for transfers between devices, on_device(): lax.psum((grad_gain_one, grad_bias_one, grad_first * sort_share, grad_sec...  199 us
    psum x1, waiting for transfers between devices, on_device(): lax.psum((grad_w_query, grad_w_key, grad_w_value, grad_w_out), 'dp')  55.9 us
    psum x1, blocking collectives, on_device(): lax.psum((grad_gain_one, grad_bias_one, grad_first * sort_share, grad_sec...  40.3 us
    all_gather x1, waiting for transfers between devices, on_device(): normed_here = lax.all_gather(normed, 'head', axis=0, tiled=True)  33.3 us
    reduce_scatter x1, waiting for transfers between devices, on_device(): lax.psum_scatter(jnp.dot(mixed_rows, w_out, preferred_element_type=jnp.fl...  31.9 us
    unnamed x327, local copies, waits for them, and re-layouts  31.9 us
    dot_general x1, matrix products, on_device(): up_value = jnp.dot(normed_two, w_up, preferred_element_type=jnp.float32)  23.5 us
    all_gather x1, waiting for transfers between devices, on_device(): lax.all_gather(grad_attention, 'head', axis=0, tiled=True)  21.4 us
  transfers between devices with their start and end apart: 6, of which 6 were waited for; matrix products, arithmetic and copies ran while one was open for 6% of the time, Pallas kernels for 0%

commit v1 on v0

--- a/solution.py
+++ b/solution.py
@@ -8,6 +8,32 @@
 ITERS = 8
 LMAX = 256
 precise = lax.Precision.HIGHEST
+
+
+def _state_targets(incoming_x, dim_at):
+    left_arr = list(incoming_x.shape[1:])
+    left_arr[dim_at] *= incoming_x.shape[0]
+    last = jnp.moveaxis(incoming_x, 0, dim_at).reshape(left_arr)
+    return last
+
+
+def _wrap_teams(target, comm_axis):
+    cores_n = lax.axis_size(comm_axis)
+    main = target[None]
+    for b in range(cores_n.bit_length() - 1):
+        far_arr = 1 << b
+        block_next = lax.ppermute(
+            main, axis_name=comm_axis, perm=tuple(((u, u ^ far_arr) for u in range(cores_n)))
+        )
+        local_now = jnp.stack([main, block_next], axis=0)
+        w2 = lax.axis_index(comm_axis) >> b & 1
+        main = jnp.where(w2 == 0, local_now, local_now[::-1]).reshape(-1, *target.shape)
+    return main
+
+
+def _feed_sectors(arr_in, sheet, ndim_at):
+    view_out = _state_targets(_wrap_teams(arr_in, sheet), ndim_at)
+    return view_out
 
 
 def smooth_gate(values):
@@ -212,7 +238,7 @@
     )
     grad_middle = cotangent.astype(jnp.float32) + grad_middle_norm
     grad_attention = grad_middle.astype(jnp.bfloat16)
-    grad_attention_here = lax.all_gather(grad_attention, "head", axis=0, tiled=True)
+    grad_attention_here = _feed_sectors(grad_attention, "head", 0)
     grad_w_out = outer_product(mixed_rows, grad_attention_here)
     grad_mixed = jnp.dot(
         grad_attention_here, out_rows.T, preferred_element_type=jnp.float32

time: 695 us -> 689 us (level)
  waiting for transfers between devices: 352 us -> 344 us
    all_gather x1 -> x0, waiting for transfers between devices: 21.4 us -> none  [on_device(): lax.all_gather(grad_attention, 'head', axis=0, tiled=True)]
    ppermute x0 -> x1, waiting for transfers between devices: none -> 14.8 us  [_wrap_teams(): lax.ppermute(main, axis_name=comm_axis, perm=tuple(((u, u ^ far_arr) for...]
where the time goes in v1:
time: 689 us; the launch traced here: 683 us
  waiting for transfers between devices  344 us (50%)
  matrix products  135 us (20%)
  local copies, waits for them, and re-layouts  80.8 us (12%)
  other arithmetic  58.6 us (9%)
  blocking collectives  47.6 us (7%)
  between operations  16.7 us (2%)
    psum x1, waiting for transfers between devices, on_device(): lax.psum((grad_gain_one, grad_bias_one, grad_first * sort_share, grad_sec...  199 us
    psum x1, waiting for transfers between devices, on_device(): lax.psum((grad_w_query, grad_w_key, grad_w_value, grad_w_out), 'dp')  54.9 us
    psum x1, blocking collectives, on_device(): lax.psum((grad_gain_one, grad_bias_one, grad_first * sort_share, grad_sec...  40.3 us
    unnamed x327, local copies, waits for them, and re-layouts  33.9 us
    all_gather x1, waiting for transfers between devices, on_device(): normed_here = lax.all_gather(normed, 'head', axis=0, tiled=True)  33.3 us
    reduce_scatter x1, waiting for transfers between devices, on_device(): lax.psum_scatter(jnp.dot(mixed_rows, w_out, preferred_element_type=jnp.fl...  31.9 us
    dot_general x1, matrix products, on_device(): up_value = jnp.dot(normed_two, w_up, preferred_element_type=jnp.float32)  22 us
    dot_general x6, matrix products, outer_product(): lax.dot_general(left, right, (((0,), (0,)), ((), ())), preferred_element_...  17.1 us
  transfers between devices with their start and end apart: 6, of which 6 were waited for; matrix products, arithmetic and copies ran while one was open for 6% of the time, Pallas kernels for 0%

profile of v1, /device:TPU:0, one launch (start us, length us, event | category | flops | bytes accessed | tf_op | source)
XLA Modules:
  0.0 682.6 jit_solution(13769608445741328147)
XLA Ops:
  16.0 33.3 %all-gather.2.cloned.1.call-done = bf16[2048,512]{1,0:T(8,128)(2,1)} async-done(((bf16[1024,512]{1,0:T(8,128)(2,1)}), bf16[2048,512]{1,0:T(8,128)(2,1)}) %all-gather.2.cloned.1.call-update) | async-done | bytes 2097168 | tf_op jit(solution)/shard_map/all_gather | solution.py:209
  70.4 4.9 reshape.616
  78.6 4.4 reshape.615
  87.1 4.9 copy_multiply_fusion.1
  115.4 31.9 %reduce-scatter.3.cloned.1.call-done = bf16[1024,512]{1,0:T(8,128)(2,1)} async-done(((bf16[2048,512]{1,0:T(8,128)(2,1)}), bf16[1024,512]{1,0:T(8,128)(2,1)}) %reduce-scatter.3.cloned.1.call-update) | async-done | bytes 1048592 | tf_op jit(solution)/shard_map/reduce_scatter | solution.py:215
  150.9 22.0 %multiply_convert_fusion = (bf16[1024,2048]{1,0:T(8,128)(2,1)S(1)}, f32[1024,2048]{1,0:T(8,128)S(1)}, f32[1024,2048]{1,0:T(8,128)}) fusion(bf16[512,2048]{1,0:T(8,128)(2,1)S(1)} %copy-done, bf16[1024,512]{1,0:T(8,128)(2,1)S(1)} %copy-done.29, bf16[1024,512]{1,0:T(8,128)(2,1)S(1)} %copy-done.2, f32[512]{0:T(512)S(1)} %copy-done.157, f32[512]{0:T(512)S(1)} %copy-done.152, ...), kind=kOutput, calls=%fused_computation.12 | convolution fusion | flops 2287992832 | bytes 25178112 | tf_op jit(solution)/shard_map/dot_general | solution.py:224
  172.9 8.4 %fusion.5 = bf16[1024,2048]{1,0:T(8,128)(2,1)S(1)} fusion(f32[1024,2048]{1,0:T(8,128)S(1)} %get-tuple-element.86, f32[1024,2048]{1,0:T(8,128)} %get-tuple-element.110, bf16[1024,512]{1,0:T(8,128)(2,1)S(1)} %copy-done.28, bf16[2048,512]{1,0:T(8,128)(2,1)S(1)} %copy-done.156), kind=kOutput, calls=%fused_computation.8 | convolution fusion | flops 2181038080 | bytes 24117248 | tf_op jit(solution)/shard_map/dot_general | solution.py:230
  186.9 4.4 fusion.167
  192.0 4.6 fusion.143
  196.6 14.8 %collective-permute-done = bf16[1,1024,512]{2,1,0:T(8,128)(2,1)S(1)} collective-permute-done((bf16[1,1024,512]{2,1,0:T(8,128)(2,1)S(1)}, bf16[1,1024,512]{2,1,0:T(8,128)(2,1)S(1)}, u32[]{:S(2)}, u32[]{:S(2)}) %collective-permute-start) | collective-permute-done | bytes 1048608 | tf_op jit(solution)/shard_map/ppermute | solution.py:25
  214.1 4.4 reshape.617
  221.6 7.2 %multiply_reduce_fusion = (f32[8,8,4,32]{3,2,1,0:T(4,128)S(1)}, f32[8,8,4,32,64]{4,3,2,1,0:T(8,128)S(1)}) fusion(f32[8,8,4,32,64]{4,3,2,1,0:T(8,128)S(1)} %copy-done.4, f32[8,8,4,32]{3,2,1,0:T(4,128)} %bitcast.112, pred[8,8,32,64]{3,2,1,0:T(8,128)(4,1)S(1)} %broadcast_or_fusion, bf16[8,8,64,4,64]{4,1,3,2,0:T(8,128)(2,1)} %copy-done.38, ...), kind=kOutput, calls=%fused_computation.47 | convolution fusion | flops 69722112 | bytes 7536640 | tf_op jit(solution)/shard_map/cibhd,cikhd->cihbk/dot_general | solution.py:107
  228.8 6.0 convolution_bitcast_fusion
  243.9 6.4 fusion.65
  250.3 7.6 %fusion.24 = f32[8,8,32,4,64]{4,1,3,2,0:T(8,128)} fusion(f32[8,8,32,4,64]{4,2,3,1,0:T(8,128)S(1)} %slice.17, f32[8,8,8]{2,1,0:T(8,128)S(1)} %get-tuple-element.88, f32[8,8]{1,0:T(8,128)S(1)} %log_add_fusion.1, f32[8,8]{1,0:T(8,128)S(1)} %log_add_fusion.2), kind=kOutput, calls=%fused_computation.42 | convolution fusion | flops 50332672 | bytes 4196864 | tf_op jit(solution)/shard_map/cij,cithd->cjthd/dot_general | solution.py:131
  269.6 7.2 %fusion.22 = f32[8,8,32,4,64]{4,1,3,2,0:T(8,128)} fusion(f32[8,8,32,4,64]{4,2,3,1,0:T(8,128)S(1)} %slice.19, f32[8,8,8]{2,1,0:T(8,128)S(1)} %get-tuple-element.88, f32[8,8]{1,0:T(8,128)S(1)} %log_add_fusion.1, f32[8,8]{1,0:T(8,128)S(1)} %log_add_fusion.2), kind=kOutput, calls=%fused_computation.40 | convolution fusion | flops 50332672 | bytes 4196864 | tf_op jit(solution)/shard_map/cij,cithd->cjthd/dot_general | solution.py:134
  276.8 5.5 fusion.75
  282.3 7.3 %psum.91 = f32[8,8,8]{2,1,0:T(8,128)S(1)} all-reduce(f32[8,8,8]{2,1,0:T(8,128)S(1)} %fusion.75), channel_id=1, replica_groups=mesh['dp'=16,'head'=2] {'head'}, use_global_device_ids=true, to_apply=%region_44.45 | all-reduce | flops 512 | bytes 4096 | tf_op jit(solution)/shard_map/psum | solution.py:249
  289.6 12.7 %fusion.14 = (bf16[8,8,32,4,64]{4,2,3,1,0:T(8,128)(2,1)S(1)}, bf16[8,8,32,4,64]{4,2,3,1,0:T(8,128)(2,1)}) fusion(f32[8,8,64,4,64]{4,2,3,1,0:T(8,128)} %convolution_bitcast_fusion, f32[8,8,32,4,64]{4,1,3,2,0:T(8,128)} %fusion.22, f32[8,8,32]{2,1,0:T(8,128)S(1)} %get-tuple-element.101, f32[8,8,32,4,64]{4,1,3,2,0:T(8,128)} %fusion.24, ...), kind=kLoop, calls=%fused_computation.28 | loop fusion | flops 3145728 | bytes 10493952 | tf_op jit(solution)/shard_map/convert_element_type | solution.py:141
  340.2 6.3 add_convert_fusion.2
  348.2 9.9 %reduce-scatter.5.cloned.1.call-done = bf16[1024,512]{1,0:T(8,128)(2,1)} async-done(((bf16[2048,512]{1,0:T(8,128)(2,1)}), bf16[1024,512]{1,0:T(8,128)(2,1)}) %reduce-scatter.5.cloned.1.call-update) | async-done | bytes 1048592 | tf_op jit(solution)/shard_map/reduce_scatter | solution.py:263
  363.0 40.3 %all-reduce = (f32[512]{0:T(512)}, f32[512]{0:T(512)}, f32[512,8]{0,1:T(8,128)}, f32[512]{0:T(512)}, f32[512]{0:T(512)}) all-reduce(f32[512]{0:T(512)S(1)} %get-tuple-element.16, f32[512]{0:T(512)S(1)} %get-tuple-element.19, f32[512,8]{0,1:T(8,128)S(1)} %fusion.80, ...), channel_id=1, replica_groups=mesh['dp'=16,'head'=2] {'dp','head'}, use_global_device_ids=true, to_apply=%region_96.97 | all-reduce | flops 6144 | bytes 49152 | tf_op jit(solution)/shard_map/psum | solution.py:279
  406.6 54.9 %all-reduce.8.cloned.1.call-done = (f32[512,256]{1,0:T(8,128)}, f32[512,256]{1,0:T(8,128)}, f32[512,256]{1,0:T(8,128)}, f32[256,512]{1,0:T(8,128)}) async-done(((f32[512,256]{1,0:T(8,128)}, f32[512,256]{1,0:T(8,128)}, f32[512,256]{1,0:T(8,128)}, f32[256,512]{1,0:T(8,128)}), (f32[512,256]{1,0:T(8,128)}, f32[512,256]{1,0:T(8,128)}, f32[512,256]{1,0:T(8,128)}, ...) | async-done | bytes 2097168 | tf_op jit(solution)/shard_map/psum | solution.py:274
  461.4 198.8 %all-reduce.6.cloned.1.call-done = (f32[512,512]{1,0:T(8,128)}, f32[512,2048]{1,0:T(8,128)}, f32[2048,512]{1,0:T(8,128)}) async-done(((f32[512,512]{1,0:T(8,128)}, f32[512,2048]{1,0:T(8,128)}, f32[2048,512]{1,0:T(8,128)}), (f32[512,512]{1,0:T(8,128)}, f32[512,2048]{1,0:T(8,128)}, f32[2048,512]{1,0:T(8,128)})) %all-reduce.6.cloned.1.call-update) | async-done | bytes 9437200 | tf_op jit(solution)/shard_map/psum | solution.py:279
  (526 shorter events, 157.8 us)
Async XLA Ops:
  7.2 143.6 %copy-start = (bf16[512,2048]{1,0:T(8,128)(2,1)S(1)}, bf16[512,2048]{1,0:T(8,128)(2,1)}, u32[]{:S(2)}) copy-start(bf16[512,2048]{1,0:T(8,128)(2,1)} %param.27) | copy-start | bytes 6291460
  7.2 45.0 %copy-start.53 = (bf16[512,512]{1,0:T(8,128)(2,1)S(1)}, bf16[512,512]{1,0:T(8,128)(2,1)}, u32[]{:S(2)}) copy-start(bf16[512,512]{1,0:T(8,128)(2,1)} %param.23) | copy-start | bytes 1572868
  7.2 42.1 %all-gather.2.cloned.1.call-start = ((), (), s32[]{:S(2)}) async-start(), calls=%async_computation.2 | async-start | bytes 3145728 | tf_op jit(solution)/shard_map/all_gather | solution.py:209
  8.9 44.3 %copy-start.150 = (bf16[512,8]{0,1:T(8,128)(2,1)S(1)}, bf16[512,8]{0,1:T(8,128)(2,1)}, u32[]{:S(2)}) copy-start(bf16[512,8]{0,1:T(8,128)(2,1)} %param.24) | copy-start | bytes 24580
  8.9 40.4 %copy-start.71 = (f32[1024]{0:T(1024)}, f32[1024]{0:T(1024)S(1)}, u32[]{:S(2)}) copy-start(f32[1024]{0:T(1024)S(1)} %broadcast_multiply_fusion.1) | copy-start | bytes 12292
  10.6 38.7 %copy-start.114 = (f32[1024]{0:T(1024)}, f32[1024]{0:T(1024)S(1)}, u32[]{:S(2)}) copy-start(f32[1024]{0:T(1024)S(1)} %fusion.45) | copy-start | bytes 12292
  10.6 38.7 %copy-start.110 = (f32[1024]{0:T(1024)}, f32[1024]{0:T(1024)S(1)}, u32[]{:S(2)}) copy-start(f32[1024]{0:T(1024)S(1)} %fusion.127) | copy-start | bytes 12292
  13.3 134.1 %reduce-scatter.3.cloned.1.call-start = ((), (), s32[]{:S(2)}) async-start(), calls=%async_computation.3 | async-start | bytes 3145728 | tf_op jit(solution)/shard_map/reduce_scatter | solution.py:215
  13.5 276.1 %copy-start.51 = (f32[8,8,32]{2,1,0:T(8,128)}, f32[8,8,32]{2,1,0:T(8,128)S(1)}, u32[]{:S(2)}) copy-start(f32[8,8,32]{2,1,0:T(8,128)S(1)} %get-tuple-element.101) | copy-start | bytes 24580
  49.3 18.4 %copy-start.5 = (bf16[2048,512]{1,0:T(8,128)(2,1)S(1)}, bf16[2048,512]{1,0:T(8,128)(2,1)}, u32[]{:S(2)}) copy-start(bf16[2048,512]{1,0:T(8,128)(2,1)} %all-gather.2.cloned.1.call-done) | copy-start | bytes 6291460
  52.6 22.6 %copy-start.55 = (f32[8,8,512]{2,1,0:T(8,128)}, f32[8,8,512]{2,1,0:T(8,128)S(1)}, u32[]{:S(2)}) copy-start(f32[8,8,512]{2,1,0:T(8,128)S(1)} %get-tuple-element.105) | copy-start | bytes 393220
  53.1 22.2 %copy-start.57 = (f32[8,8,512]{2,1,0:T(8,128)}, f32[8,8,512]{2,1,0:T(8,128)S(1)}, u32[]{:S(2)}) copy-start(f32[8,8,512]{2,1,0:T(8,128)S(1)} %fusion.85) | copy-start | bytes 393220
  58.0 17.2 %copy-start.22 = (f32[8,8,8]{2,1,0:T(8,128)}, f32[8,8,8]{2,1,0:T(8,128)S(1)}, u32[]{:S(2)}) copy-start(f32[8,8,8]{2,1,0:T(8,128)S(1)} %get-tuple-element.94) | copy-start | bytes 6148
  61.0 14.3 %copy-start.24 = (f32[8,8,8]{2,1,0:T(8,128)}, f32[8,8,8]{2,1,0:T(8,128)S(1)}, u32[]{:S(2)}) copy-start(f32[8,8,8]{2,1,0:T(8,128)S(1)} %get-tuple-element.92) | copy-start | bytes 6148
  107.6 39.8 %copy-start.2 = (bf16[1024,512]{1,0:T(8,128)(2,1)S(1)}, bf16[1024,512]{1,0:T(8,128)(2,1)}, u32[]{:S(2)}) copy-start(bf16[1024,512]{1,0:T(8,128)(2,1)} %param.15) | copy-start | bytes 3145732
  112.0 38.8 %copy-start.152 = (f32[512]{0:T(512)S(1)}, f32[512]{0:T(512)}, u32[]{:S(2)}) copy-start(f32[512]{0:T(512)} %param.25) | copy-start | bytes 6148
  112.0 38.8 %copy-start.157 = (f32[512]{0:T(512)S(1)}, f32[512]{0:T(512)}, u32[]{:S(2)}) copy-start(f32[512]{0:T(512)} %param.26) | copy-start | bytes 6148
  115.4 242.8 %reduce-scatter.5.cloned.1.call-start = ((), (), s32[]{:S(2)}) async-start(), calls=%async_computation.4 | async-start | bytes 3145728 | tf_op jit(solution)/shard_map/reduce_scatter | solution.py:263
  150.8 22.1 %copy-start.28 = (bf16[1024,512]{1,0:T(8,128)(2,1)S(1)}, bf16[1024,512]{1,0:T(8,128)(2,1)}, u32[]{:S(2)}) copy-start(bf16[1024,512]{1,0:T(8,128)(2,1)} %param.29) | copy-start | bytes 3145732
  150.8 22.0 %copy-start.156 = (bf16[2048,512]{1,0:T(8,128)(2,1)S(1)}, bf16[2048,512]{1,0:T(8,128)(2,1)}, u32[]{:S(2)}) copy-start(bf16[2048,512]{1,0:T(8,128)(2,1)} %param.28) | copy-start | bytes 6291460
  186.5 25.0 %collective-permute-start = (bf16[1,1024,512]{2,1,0:T(8,128)(2,1)S(1)}, bf16[1,1024,512]{2,1,0:T(8,128)(2,1)S(1)}, u32[]{:S(2)}, u32[]{:S(2)}) collective-permute-start(bf16[1,1024,512]{2,1,0:T(8,128)(2,1)S(1)} %fusion.209), channel_id=1, source_target_pairs={{0,1},{1,0},{2,3},{3,2},{4,5},{5,4},{6,7},{7,6},{8,9},{9,8},{10,11... | collective-permute-start | bytes 3145736 | tf_op jit(solution)/shard_map/ppermute | solution.py:25
  325.1 136.3 %all-reduce.8.cloned.1.call-start = ((), (), s32[]{:S(2)}) async-start(), calls=%async_computation.6 | async-start | bytes 4194304 | tf_op jit(solution)/shard_map/psum | solution.py:274
  334.7 325.6 %all-reduce.6.cloned.1.call-start = ((), (), s32[]{:S(2)}) async-start(), calls=%async_computation.5 | async-start | bytes 18874368 | tf_op jit(solution)/shard_map/psum | solution.py:279
  359.4 43.9 %copy-start.9 = (f32[1024,512]{1,0:T(8,128)S(1)}, f32[1024,512]{1,0:T(8,128)}, u32[]{:S(2)}) copy-start(f32[1024,512]{1,0:T(8,128)} %copy-done.8) | copy-start | bytes 6291460
  (143 other events, 640.4 us)
Sparse Core Ops, SparseCore 0:
  13.4 35.8 all-gather.1
  115.5 31.8 reduce-scatter.2
  325.2 32.8 reduce-scatter.4
  362.6 98.8 all-reduce.7
  469.0 191.2 all-reduce.5
